TPU v7x, 512 devices: a whole 4x8x8 slice. The times are simulated.
512 devices in a mesh: dp: 8 (over y), pipe: 4 (over z_lo), tensor: 16 (over z_hi, x, core).
Axes of the slice: x: 4, y: 8, z: 8 (z_hi: 2, z_lo: 4; z = z_hi * 4 + z_lo), core: 2. Of those that a mesh axis runs over, the one named last changes fastest.
Arguments:
- activations: bfloat16 [4, 1536, 4096], P('pipe', 'tensor', 'dp'), may hold values from -6 to 6
- upstream: bfloat16 [4, 1536, 4096], P('pipe', 'tensor', 'dp'), may hold values from -4 to 4
- gate_value: bfloat16 [4, 1536, 14336], P('pipe', 'dp', 'tensor'), may hold values from -6 to 6
- up_value: bfloat16 [4, 1536, 14336], P('pipe', 'dp', 'tensor'), may hold values from -6 to 6
- hidden_grad: bfloat16 [4, 1536, 14336], P('pipe', 'dp', 'tensor'), may hold values from -4 to 4
- gate_weight: bfloat16 [4, 4096, 14336], P('pipe', 'dp', 'tensor'), may hold values from -0.09375 to 0.09375
- up_weight: bfloat16 [4, 4096, 14336], P('pipe', 'dp', 'tensor'), may hold values from -0.09375 to 0.09375
- gate_mask: int32 [4, 32, 112], P('pipe', 'dp', 'tensor'), may hold values 0 or 1
- up_mask: int32 [4, 32, 112], P('pipe', 'dp', 'tensor'), may hold values 0 or 1
Outputs:
- gate_gradient: bfloat16 [4, 4096, 14336], P('pipe', 'dp', 'tensor')
- up_gradient: bfloat16 [4, 4096, 14336], P('pipe', 'dp', 'tensor')
- handed_back: bfloat16 [4, 1536, 4096], P('pipe', 'tensor', 'dp')
Inputs may be any that keep to these rules, and one draw needn't show every extreme that they name: gate_mask[s, i, j] keeps (1) or prunes (0) block (i, j) of gate_weight[s]. up_mask[s, i, j] keeps (1) or prunes (0) block (i, j) of up_weight[s].
All inputs are finite; a program needn't handle non-finite values.
Results may differ from a plain program's by a relative error of at most 0.0049.
Values may be sent and summed in bfloat16 or wider, within the bound.
A program may use at most 64 MiB of HBM per device.

v0:
```python
import jax
import jax.numpy as jnp
from jax import lax
from jax.sharding import PartitionSpec as P


def shifted(array, axis, by):
    devices = lax.axis_size(axis)
    pairs = [(i, i + by) for i in range(devices) if 0 <= i + by < devices]
    return lax.ppermute(array, axis, pairs)


def apply_blocks(matrix, keep_mask):
    rows_blocks, cols_blocks = keep_mask.shape
    shaped = matrix.reshape(
        rows_blocks, matrix.shape[0] // rows_blocks, cols_blocks, matrix.shape[1] // cols_blocks
    )
    return (shaped * keep_mask.astype(matrix.dtype)[:, None, :, None]).reshape(matrix.shape)


def per_device(
    activations,
    upstream,
    gate_value,
    up_value,
    hidden_grad,
    gate_weight,
    up_weight,
    gate_mask,
    up_mask,
):
    gathered = lax.all_gather(activations, "tensor", axis=1, tiled=True)[0]
    gate_float = gate_value[0].astype(jnp.float32)
    up_float = up_value[0].astype(jnp.float32)
    hidden_float = hidden_grad[0].astype(jnp.float32)
    gate_sigmoid = jax.nn.sigmoid(gate_float)
    up_delta = (hidden_float * gate_float * gate_sigmoid).astype(jnp.bfloat16)
    gate_delta = (
        hidden_float * up_float * gate_sigmoid * (1.0 + gate_float * (1.0 - gate_sigmoid))
    ).astype(jnp.bfloat16)
    gate_kept = apply_blocks(gate_weight[0], gate_mask[0])
    up_kept = apply_blocks(up_weight[0], up_mask[0])
    over_tokens = (((0,), (0,)), ((), ()))
    over_hidden = (((1,), (1,)), ((), ()))
    gate_piece = lax.all_gather(gate_delta, "dp", axis=0, tiled=True)
    up_piece = lax.all_gather(up_delta, "dp", axis=0, tiled=True)
    gate_acc = lax.dot_general(
        gathered, gate_piece, over_tokens, preferred_element_type=jnp.float32
    )
    up_acc = lax.dot_general(gathered, up_piece, over_tokens, preferred_element_type=jnp.float32)
    partial_rows = lax.dot_general(
        gate_piece, gate_kept, over_hidden, preferred_element_type=jnp.float32
    )
    partial_rows = partial_rows + lax.dot_general(
        up_piece, up_kept, over_hidden, preferred_element_type=jnp.float32
    )
    branch = partial_rows
    gate_acc, up_acc, branch = (gate_acc, up_acc, branch)
    own_rows = lax.psum_scatter(branch, "tensor", scatter_dimension=0, tiled=True)
    gate_gradient = apply_blocks(gate_acc, gate_mask[0]).astype(jnp.bfloat16)[None]
    up_gradient = apply_blocks(up_acc, up_mask[0]).astype(jnp.bfloat16)[None]
    section_grad = (upstream[0].astype(jnp.float32) + own_rows).astype(jnp.bfloat16)
    handed = shifted(section_grad, "pipe", -1)
    return (gate_gradient, up_gradient, handed[None])


def solution(mesh):
    return jax.shard_map(
        per_device,
        mesh=mesh,
        in_specs=(
            P("pipe", "tensor", "dp"),
            P("pipe", "tensor", "dp"),
            P("pipe", "dp", "tensor"),
            P("pipe", "dp", "tensor"),
            P("pipe", "dp", "tensor"),
            P("pipe", "dp", "tensor"),
            P("pipe", "dp", "tensor"),
            P("pipe", "dp", "tensor"),
            P("pipe", "dp", "tensor"),
        ),
        out_specs=(P("pipe", "dp", "tensor"), P("pipe", "dp", "tensor"), P("pipe", "tensor", "dp")),
        check_vma=False,
    )
```

profile of v0, /device:TPU:64, one launch (start us, length us, event | category | flops | bytes accessed | tf_op | source)
XLA Modules:
  0.0 296.9 jit_solution(10414191053938637605)
XLA Ops:
  7.2 0.0 copy-start
  7.2 0.0 copy-start.3
  7.2 0.0 copy-start.1
  7.2 0.0 all-gather.4.cloned.1.call-start
  7.2 2.5 fusion.29
  9.8 0.0 all-gather.4.cloned.1.call-update
  9.8 0.0 all-gather.8.cloned.1.call-start
  9.8 0.7 all-gather.8.cloned.1.call-update
  10.5 0.0 all-gather.6.cloned.1.call-start
  10.6 0.7 all-gather.6.cloned.1.call-update
  11.3 0.0 reduce-scatter.2.cloned.1.call-start
  11.3 0.8 convert_bitcast_fusion.3
  12.1 0.1 copy.19
  12.2 0.0 copy-done
  12.2 0.5 copy.18
  12.7 0.0 copy-done.3
  12.7 0.1 copy.21
  12.8 0.0 copy-done.1
  12.9 0.5 copy.20
  13.4 46.9 %all-gather.4.cloned.1.call-done = bf16[1536,896]{1,0:T(8,128)(2,1)} async-done(((bf16[192,896]{1,0:T(8,128)(2,1)}), bf16[1536,896]{1,0:T(8,128)(2,1)}) %all-gather.4.cloned.1.call-update) | async-done | bytes 2752528 | tf_op jit(solution)/shard_map/all_gather | solution.py:45
  60.3 0.3 mul.74
  60.6 5.3 %fusion.17 = f32[1536,512]{1,0:T(8,128)} fusion(bf16[1536,896]{1,0:T(8,128)(2,1)} %all-gather.4.cloned.1.call-done, bf16[112,8,4,128]{3,2,1,0:T(4,128)(2,1)S(1)} %bitcast.99, bf16[1,512,896]{1,2,0:T(8,128)(2,1)S(1)} %copy.18), kind=kOutput, calls=%fused_computation.17 | convolution fusion | flops 1409744896 | bytes 7733248 | tf_op jit(solution)/shard_map/dot_general | solution.py:51
  65.8 41.5 %all-gather.8.cloned.1.call-done = bf16[1536,896]{1,0:T(8,128)(2,1)} async-done(((bf16[192,896]{1,0:T(8,128)(2,1)}), bf16[1536,896]{1,0:T(8,128)(2,1)}) %all-gather.8.cloned.1.call-update) | async-done | bytes 2752528 | tf_op jit(solution)/shard_map/all_gather | solution.py:46
  107.3 0.3 mul.77
  107.6 6.2 %convolution_add_fusion = f32[1536,512]{1,0:T(8,128)} fusion(f32[1536,512]{1,0:T(8,128)} %fusion.17, bf16[1536,896]{1,0:T(8,128)(2,1)} %all-gather.8.cloned.1.call-done, bf16[112,8,4,128]{3,2,1,0:T(4,128)(2,1)S(1)} %bitcast.98, bf16[1,512,896]{1,2,0:T(8,128)(2,1)S(1)} %copy.20), kind=kOutput, calls=%fused_computation | convolution fusion | flops 1410531328 | bytes 10878976 | tf_op jit(solution)/shard_map/dot_general | solution.py:54
  113.8 0.0 reduce-scatter.2.cloned.1.call-update
  113.9 0.1 copy.16
  114.0 0.1 copy.17
  114.1 58.1 %all-gather.6.cloned.1.call-done = bf16[1,1536,512]{2,1,0:T(8,128)(2,1)} async-done(((bf16[1,96,512]{2,1,0:T(8,128)(2,1)}), bf16[1,1536,512]{2,1,0:T(8,128)(2,1)}) %all-gather.6.cloned.1.call-update) | async-done | bytes 1572880 | tf_op jit(solution)/shard_map/all_gather | solution.py:32
  172.2 0.3 mul.66
  172.5 0.0 copy-start.2
  172.5 3.9 %fusion.10 = bf16[1,512,896]{1,2,0:T(8,128)(2,1)S(1)} fusion(f32[112,8,4,128]{3,2,1,0:T(4,128)S(1)} %bitcast.97, bf16[1536,896]{1,0:T(8,128)(2,1)} %all-gather.4.cloned.1.call-done, bf16[1,1536,512]{2,1,0:T(8,128)(2,1)} %all-gather.6.cloned.1.call-done), kind=kOutput, calls=%fused_computation.9 | convolution fusion | flops 1410203648 | bytes 7077888 | tf_op jit(solution)/shard_map/dot_general | solution.py:47
  176.4 100.5 %reduce-scatter.2.cloned.1.call-done = f32[96,512]{1,0:T(8,128)} async-done(((f32[1536,512]{1,0:T(8,128)}), f32[96,512]{1,0:T(8,128)}) %reduce-scatter.2.cloned.1.call-update) | async-done | bytes 196624 | tf_op jit(solution)/shard_map/reduce_scatter | solution.py:59
  276.9 0.0 copy-done.2
  276.9 0.9 fusion.30
  277.9 5.2 %collective-permute-start = (bf16[96,512]{1,0:T(8,128)(2,1)S(1)}, bf16[96,512]{1,0:T(8,128)(2,1)S(1)}, u32[]{:S(2)}, u32[]{:S(2)}) collective-permute-start(bf16[96,512]{1,0:T(8,128)(2,1)S(1)} %fusion.30), channel_id=1, source_target_pairs={{16,0},{32,16},{48,32},{17,1},{33,17},{49,33},{18,2},{34,18},{50,3... | collective-permute-start | bytes 294920 | tf_op jit(solution)/shard_map/ppermute | solution.py:10
  283.1 0.3 mul.71
  283.4 3.8 %fusion.13 = bf16[1,512,896]{1,2,0:T(8,128)(2,1)S(1)} fusion(f32[112,8,4,128]{3,2,1,0:T(4,128)S(1)} %bitcast.96, bf16[1536,896]{1,0:T(8,128)(2,1)} %all-gather.8.cloned.1.call-done, bf16[1,1536,512]{2,1,0:T(8,128)(2,1)} %all-gather.6.cloned.1.call-done), kind=kOutput, calls=%fused_computation.10 | convolution fusion | flops 1410203648 | bytes 7077888 | tf_op jit(solution)/shard_map/dot_general | solution.py:50
  287.2 1.3 copy.22
  288.5 1.3 copy.23
  289.8 0.0 collective-permute-done
  289.8 0.6 copy.43
  (1 shorter events, 0.0 us)
Async XLA Ops:
  7.2 5.0 %copy-start = (bf16[1,512,896]{2,1,0:T(8,128)(2,1)S(1)}, bf16[1,512,896]{2,1,0:T(8,128)(2,1)}, u32[]{:S(2)}) copy-start(bf16[1,512,896]{2,1,0:T(8,128)(2,1)} %param.14) | copy-start | bytes 2752516
  7.2 5.5 %copy-start.3 = (s32[1,4,7]{2,1,0:T(4,128)S(1)}, s32[1,4,7]{2,1,0:T(4,128)}, u32[]{:S(2)}) copy-start(s32[1,4,7]{2,1,0:T(4,128)} %param.17) | copy-start | bytes 340
  7.2 5.7 %copy-start.1 = (bf16[1,512,896]{2,1,0:T(8,128)(2,1)S(1)}, bf16[1,512,896]{2,1,0:T(8,128)(2,1)}, u32[]{:S(2)}) copy-start(bf16[1,512,896]{2,1,0:T(8,128)(2,1)} %param.15) | copy-start | bytes 2752516
  7.2 53.1 %all-gather.4.cloned.1.call-start = ((), (), s32[]{:S(2)}) async-start(), calls=%async_computation.1 | async-start | bytes 3096576 | tf_op jit(solution)/shard_map/all_gather | solution.py:45
  9.8 97.5 %all-gather.8.cloned.1.call-start = ((), (), s32[]{:S(2)}) async-start(), calls=%async_computation.3 | async-start | bytes 3096576 | tf_op jit(solution)/shard_map/all_gather | solution.py:46
  10.5 161.7 %all-gather.6.cloned.1.call-start = ((), (), s32[]{:S(2)}) async-start(), calls=%async_computation.2 | async-start | bytes 1671168 | tf_op jit(solution)/shard_map/all_gather | solution.py:32
  11.3 265.7 %reduce-scatter.2.cloned.1.call-start = ((), (), s32[]{:S(2)}) async-start(), calls=%async_computation.4 | async-start | bytes 3342336 | tf_op jit(solution)/shard_map/reduce_scatter | solution.py:59
  172.5 104.4 %copy-start.2 = (bf16[1,96,512]{2,1,0:T(8,128)(2,1)S(1)}, bf16[1,96,512]{2,1,0:T(8,128)(2,1)}, u32[]{:S(2)}) copy-start(bf16[1,96,512]{2,1,0:T(8,128)(2,1)} %param.10) | copy-start | bytes 294916
  277.9 11.9 %collective-permute-start = (bf16[96,512]{1,0:T(8,128)(2,1)S(1)}, bf16[96,512]{1,0:T(8,128)(2,1)S(1)}, u32[]{:S(2)}, u32[]{:S(2)}) collective-permute-start(bf16[96,512]{1,0:T(8,128)(2,1)S(1)} %fusion.30), channel_id=1, source_target_pairs={{16,0},{32,16},{48,32},{17,1},{33,17},{49,33},{18,2},{34,18},{50,3... | collective-permute-start | bytes 294920 | tf_op jit(solution)/shard_map/ppermute | solution.py:10
Sparse Core Ops, SparseCore 0:
  10.7 49.5 all-gather.3
  62.9 44.3 all-gather.7
  110.6 61.5 all-gather.5
  176.9 99.9 reduce-scatter.1
where the time goes:
time: 297 us
  waiting for transfers between devices  248 us (84%)
  matrix products  19.2 us (6%)
  between operations  13.9 us (5%)
  local copies, waits for them, and re-layouts  5.86 us (2%)
  starting transfers between devices  5.31 us (2%)
  other arithmetic  4.23 us (1%)
    reduce_scatter x1, waiting for transfers between devices, per_device(): lax.psum_scatter(branch, 'tensor', scatter_dimension=0, tiled=True)  101 us
    all_gather x1, waiting for transfers between devices, per_device(): gathered = lax.all_gather(activations, 'tensor', axis=1, tiled=True)[0]  58.1 us
    all_gather x1, waiting for transfers between devices, per_device(): gate_piece = lax.all_gather(gate_delta, 'dp', axis=0, tiled=True)  46.9 us
    all_gather x1, waiting for transfers between devices, per_device(): up_piece = lax.all_gather(up_delta, 'dp', axis=0, tiled=True)  41.5 us
    dot_general x1, matrix products, per_device(): lax.dot_general(up_piece, up_kept, over_hidden, preferred_element_type=jn...  6.21 us
  transfers between devices with their start and end apart: 5, of which 4 were waited for; matrix products, arithmetic and copies ran while one was open for 8% of the time, Pallas kernels for 0%

commit v1 on v0

--- a/solution.py
+++ b/solution.py
@@ -42,7 +42,13 @@
     up_kept = apply_blocks(up_weight[0], up_mask[0])
     over_tokens = (((0,), (0,)), ((), ()))
     over_hidden = (((1,), (1,)), ((), ()))
-    gate_piece = lax.all_gather(gate_delta, "dp", axis=0, tiled=True)
+    many = lax.axis_size("dp")
+    log = [gate_delta]
+    for ix in tuple(range(many - 1)):
+        log.append(lax.ppermute(log[-1], "dp", [(m, (m + 1) % many) for m in range(many)]))
+    gate_piece = jnp.roll(
+        jnp.concatenate(log[::-1], axis=0), (lax.axis_index("dp") + 1) * gate_delta.shape[0], axis=0
+    )
     up_piece = lax.all_gather(up_delta, "dp", axis=0, tiled=True)
     gate_acc = lax.dot_general(
         gathered, gate_piece, over_tokens, preferred_element_type=jnp.float32

time: 297 us -> 278 us (0.936)
  waiting for transfers between devices: 248 us -> 200 us
  local copies, waits for them, and re-layouts: 5.86 us -> 21.5 us
  starting transfers between devices: 5.31 us -> 20.2 us
    ppermute x0 -> x7, waiting for transfers between devices: none -> 76.1 us  [per_device(): lax.ppermute(log[-1], 'dp', [(m, (m + 1) % many) for m in range(many)])]
    all_gather x1 -> x0, waiting for transfers between devices: 46.9 us -> none  [per_device(): gate_piece = lax.all_gather(gate_delta, 'dp', axis=0, tiled=True)]
    all_gather x1, waiting for transfers between devices: 41.5 us -> 0.01 us  [per_device(): up_piece = lax.all_gather(up_delta, 'dp', axis=0, tiled=True)]
    all_gather x1, waiting for transfers between devices: 58.1 us -> 24.5 us  [per_device(): gathered = lax.all_gather(activations, 'tensor', axis=1, tiled=True)[0]]
    ppermute x0 -> x7, starting transfers between devices: none -> 14.9 us  [per_device(): lax.ppermute(log[-1], 'dp', [(m, (m + 1) % many) for m in range(many)])]
    unnamed x13 -> x26, local copies, waits for them, and re-layouts: 4.25 us -> 19.2 us
  transfers between devices with their start and end apart: 5 -> 11, of which waited for: 4 -> 9; matrix products, arithmetic and copies ran while one was open for 8% -> 14% of each run, Pallas kernels for 0% -> 0%
where the time goes in v1:
time: 278 us; the launch traced here: 277 us
  waiting for transfers between devices  200 us (72%)
  local copies, waits for them, and re-layouts  21.5 us (8%)
  starting transfers between devices  20.2 us (7%)
  matrix products  16.8 us (6%)
  between operations  13.9 us (5%)
  other arithmetic  4.74 us (2%)
    reduce_scatter x1, waiting for transfers between devices, per_device(): lax.psum_scatter(branch, 'tensor', scatter_dimension=0, tiled=True)  99.3 us
    ppermute x7, waiting for transfers between devices, per_device(): lax.ppermute(log[-1], 'dp', [(m, (m + 1) % many) for m in range(many)])  76.1 us
    all_gather x1, waiting for transfers between devices, per_device(): gathered = lax.all_gather(activations, 'tensor', axis=1, tiled=True)[0]  24.5 us
    unnamed x26, local copies, waits for them, and re-layouts  19.2 us
    ppermute x7, starting transfers between devices, per_device(): lax.ppermute(log[-1], 'dp', [(m, (m + 1) % many) for m in range(many)])  14.9 us
  transfers between devices with their start and end apart: 11, of which 9 were waited for; matrix products, arithmetic and copies ran while one was open for 14% of the time, Pallas kernels for 0%

profile of v1, /device:TPU:64, one launch (start us, length us, event | category | flops | bytes accessed | tf_op | source)
XLA Modules:
  0.0 277.1 jit_solution(6053736874729007396)
XLA Ops:
  7.2 2.3 fusion.35
  9.6 3.5 %collective-permute-start = (bf16[192,896]{1,0:T(8,128)(2,1)S(1)}, bf16[192,896]{1,0:T(8,128)(2,1)S(1)}, u32[]{:S(2)}, u32[]{:S(2)}) collective-permute-start(bf16[192,896]{1,0:T(8,128)(2,1)S(1)} %get-tuple-element.10), channel_id=1, source_target_pairs={{0,64},{64,128},{128,192},{192,256},{256,320},{320,384},{384,448},... | collective-permute-start | bytes 1032200 | tf_op jit(solution)/shard_map/ppermute | solution.py:48
  13.1 9.9 %collective-permute-done = bf16[192,896]{1,0:T(8,128)(2,1)S(1)} collective-permute-done((bf16[192,896]{1,0:T(8,128)(2,1)S(1)}, bf16[192,896]{1,0:T(8,128)(2,1)S(1)}, u32[]{:S(2)}, u32[]{:S(2)}) %collective-permute-start) | collective-permute-done | bytes 344096 | tf_op jit(solution)/shard_map/ppermute | solution.py:48
  23.0 1.9 collective-permute-start.1
  24.9 16.2 %collective-permute-done.1 = bf16[192,896]{1,0:T(8,128)(2,1)S(1)} collective-permute-done((bf16[192,896]{1,0:T(8,128)(2,1)S(1)}, bf16[192,896]{1,0:T(8,128)(2,1)S(1)}, u32[]{:S(2)}, u32[]{:S(2)}) %collective-permute-start.1) | collective-permute-done | bytes 344096 | tf_op jit(solution)/shard_map/ppermute | solution.py:48
  41.1 1.9 collective-permute-start.2
  43.0 17.5 %collective-permute-done.2 = bf16[192,896]{1,0:T(8,128)(2,1)S(1)} collective-permute-done((bf16[192,896]{1,0:T(8,128)(2,1)S(1)}, bf16[192,896]{1,0:T(8,128)(2,1)S(1)}, u32[]{:S(2)}, u32[]{:S(2)}) %collective-permute-start.2) | collective-permute-done | bytes 344096 | tf_op jit(solution)/shard_map/ppermute | solution.py:48
  60.5 1.9 collective-permute-start.3
  62.4 13.5 %collective-permute-done.3 = bf16[192,896]{1,0:T(8,128)(2,1)S(1)} collective-permute-done((bf16[192,896]{1,0:T(8,128)(2,1)S(1)}, bf16[192,896]{1,0:T(8,128)(2,1)S(1)}, u32[]{:S(2)}, u32[]{:S(2)}) %collective-permute-start.3) | collective-permute-done | bytes 344096 | tf_op jit(solution)/shard_map/ppermute | solution.py:48
  75.9 1.9 collective-permute-start.4
  77.8 8.4 %collective-permute-done.4 = bf16[192,896]{1,0:T(8,128)(2,1)S(1)} collective-permute-done((bf16[192,896]{1,0:T(8,128)(2,1)S(1)}, bf16[192,896]{1,0:T(8,128)(2,1)S(1)}, u32[]{:S(2)}, u32[]{:S(2)}) %collective-permute-start.4) | collective-permute-done | bytes 344096 | tf_op jit(solution)/shard_map/ppermute | solution.py:48
  86.2 1.9 collective-permute-start.5
  88.2 8.4 %collective-permute-done.5 = bf16[192,896]{1,0:T(8,128)(2,1)S(1)} collective-permute-done((bf16[192,896]{1,0:T(8,128)(2,1)S(1)}, bf16[192,896]{1,0:T(8,128)(2,1)S(1)}, u32[]{:S(2)}, u32[]{:S(2)}) %collective-permute-start.5) | collective-permute-done | bytes 344096 | tf_op jit(solution)/shard_map/ppermute | solution.py:48
  96.6 1.9 collective-permute-start.6
  98.5 0.8 convert_bitcast_fusion.2
  99.3 0.8 convert_bitcast_fusion.3
  100.1 2.2 copy.20
  102.4 2.2 copy.18
  104.6 2.3 collective-permute-done.6
  106.9 0.8 constant_dynamic-update-slice_fusion.15
  107.7 0.8 constant_dynamic-update-slice_fusion.14
  108.5 0.8 constant_dynamic-update-slice_fusion.13
  109.2 0.8 constant_dynamic-update-slice_fusion.12
  110.0 0.8 constant_dynamic-update-slice_fusion.11
  110.7 0.8 constant_dynamic-update-slice_fusion.10
  111.5 0.8 constant_dynamic-update-slice_fusion.9
  112.3 0.8 constant_dynamic-update-slice_fusion.8
  113.1 0.8 constant_dynamic-update-slice_fusion.7
  113.8 0.8 constant_dynamic-update-slice_fusion.6
  114.6 0.8 constant_dynamic-update-slice_fusion.5
  115.4 0.8 constant_dynamic-update-slice_fusion.4
  116.1 0.8 constant_dynamic-update-slice_fusion.3
  116.9 0.8 constant_dynamic-update-slice_fusion.2
  117.7 0.8 constant_dynamic-update-slice_fusion.1
  118.4 0.8 constant_dynamic-update-slice_fusion
  119.2 0.3 mul.81
  119.6 3.9 %fusion.22 = f32[1536,512]{1,0:T(8,128)S(1)} fusion(bf16[1536,896]{1,0:T(8,128)(2,1)} %all-gather.5.cloned.1.call-done, bf16[112,8,4,128]{3,2,1,0:T(4,128)(2,1)S(1)} %bitcast.97, bf16[1,512,896]{1,2,0:T(8,128)(2,1)} %copy.20), kind=kOutput, calls=%fused_computation.17 | convolution fusion | flops 1409744896 | bytes 7733248 | tf_op jit(solution)/shard_map/dot_general | solution.py:60
  123.5 0.3 mul.78
  123.8 5.5 %convolution_add_fusion = f32[1536,512]{1,0:T(8,128)} fusion(f32[1536,512]{1,0:T(8,128)S(1)} %fusion.22, bf16[3072,896]{1,0:T(8,128)(2,1)} %constant_dynamic-update-slice_fusion, s32[]{:T(128)S(6)} %select_n.14, bf16[112,8,4,128]{3,2,1,0:T(4,128)(2,1)S(1)} %bitcast.96, bf16[1,512,896]{1,2,0:T(8,128)(2,1)S(1)} %copy-done), kind=kOutput, calls=%fused_computation | convolution fusion | flops 1410531328 | bytes 10878980 | tf_op jit(solution)/shard_map/dot_general | solution.py:57
  129.5 24.5 %all-gather.3.cloned.1.call-done = bf16[1,1536,512]{2,1,0:T(8,128)(2,1)} async-done(((bf16[1,96,512]{2,1,0:T(8,128)(2,1)}), bf16[1,1536,512]{2,1,0:T(8,128)(2,1)}) %all-gather.3.cloned.1.call-update) | async-done | bytes 1572880 | tf_op jit(solution)/shard_map/all_gather | solution.py:32
  154.3 4.0 %fusion.14 = bf16[1,512,896]{1,2,0:T(8,128)(2,1)S(1)} fusion(f32[112,8,4,128]{3,2,1,0:T(4,128)S(1)} %bitcast.94, bf16[1,1536,512]{2,1,0:T(8,128)(2,1)} %all-gather.3.cloned.1.call-done, bf16[3072,896]{1,0:T(8,128)(2,1)} %constant_dynamic-update-slice_fusion, s32[]{:T(128)S(6)} %select_n.14), kind=kOutput, calls=%fused_computation.11 | convolution fusion | flops 1410203648 | bytes 7077892 | tf_op jit(solution)/shard_map/dot_general | solution.py:53
  158.3 1.3 copy.22
  159.5 99.3 %reduce-scatter.2.cloned.1.call-done = f32[96,512]{1,0:T(8,128)} async-done(((f32[1536,512]{1,0:T(8,128)}), f32[96,512]{1,0:T(8,128)}) %reduce-scatter.2.cloned.1.call-update) | async-done | bytes 196624 | tf_op jit(solution)/shard_map/reduce_scatter | solution.py:65
  258.8 0.9 fusion.36
  259.8 5.2 %collective-permute-start.7 = (bf16[96,512]{1,0:T(8,128)(2,1)S(1)}, bf16[96,512]{1,0:T(8,128)(2,1)S(1)}, u32[]{:S(2)}, u32[]{:S(2)}) collective-permute-start(bf16[96,512]{1,0:T(8,128)(2,1)S(1)} %fusion.36), channel_id=1, source_target_pairs={{16,0},{32,16},{48,32},{17,1},{33,17},{49,33},{18,2},{34,18},{50,3... | collective-permute-start | bytes 294920 | tf_op jit(solution)/shard_map/ppermute | solution.py:10
  265.3 3.4 %fusion.19 = bf16[1,512,896]{1,2,0:T(8,128)(2,1)S(1)} fusion(f32[112,8,4,128]{3,2,1,0:T(4,128)S(1)} %bitcast.95, bf16[1536,896]{1,0:T(8,128)(2,1)} %all-gather.5.cloned.1.call-done, bf16[1,1536,512]{2,1,0:T(8,128)(2,1)S(1)} %copy-done.2), kind=kOutput, calls=%fused_computation.12 | convolution fusion | flops 1410203648 | bytes 7077888 | tf_op jit(solution)/shard_map/dot_general | solution.py:56
  268.7 1.3 copy.23
  270.0 0.6 copy.58
  (20 shorter events, 1.2 us)
Async XLA Ops:
  7.2 112.1 %all-gather.5.cloned.1.call-start = ((), (), s32[]{:S(2)}) async-start(), calls=%async_computation.2 | async-start | bytes 3096576 | tf_op jit(solution)/shard_map/all_gather | solution.py:52
  9.5 144.4 %all-gather.3.cloned.1.call-start = ((), (), s32[]{:S(2)}) async-start(), calls=%async_computation.1 | async-start | bytes 1671168 | tf_op jit(solution)/shard_map/all_gather | solution.py:32
  9.6 13.4 %collective-permute-start = (bf16[192,896]{1,0:T(8,128)(2,1)S(1)}, bf16[192,896]{1,0:T(8,128)(2,1)S(1)}, u32[]{:S(2)}, u32[]{:S(2)}) collective-permute-start(bf16[192,896]{1,0:T(8,128)(2,1)S(1)} %get-tuple-element.10), channel_id=1, source_target_pairs={{0,64},{64,128},{128,192},{192,256},{256,320},{320,384},{384,448},... | collective-permute-start | bytes 1032200 | tf_op jit(solution)/shard_map/ppermute | solution.py:48
  23.0 18.1 %collective-permute-start.1 = (bf16[192,896]{1,0:T(8,128)(2,1)S(1)}, bf16[192,896]{1,0:T(8,128)(2,1)S(1)}, u32[]{:S(2)}, u32[]{:S(2)}) collective-permute-start(bf16[192,896]{1,0:T(8,128)(2,1)S(1)} %collective-permute-done), channel_id=1, source_target_pairs={{0,64},{64,128},{128,192},{192,256},{256,320},{320,384},{384,448},... | collective-permute-start | bytes 1032200 | tf_op jit(solution)/shard_map/ppermute | solution.py:48
  41.1 19.4 %collective-permute-start.2 = (bf16[192,896]{1,0:T(8,128)(2,1)S(1)}, bf16[192,896]{1,0:T(8,128)(2,1)S(1)}, u32[]{:S(2)}, u32[]{:S(2)}) collective-permute-start(bf16[192,896]{1,0:T(8,128)(2,1)S(1)} %collective-permute-done.1), channel_id=1, source_target_pairs={{0,64},{64,128},{128,192},{192,256},{256,320},{320,384},{384,448},... | collective-permute-start | bytes 1032200 | tf_op jit(solution)/shard_map/ppermute | solution.py:48
  60.5 15.4 %collective-permute-start.3 = (bf16[192,896]{1,0:T(8,128)(2,1)S(1)}, bf16[192,896]{1,0:T(8,128)(2,1)S(1)}, u32[]{:S(2)}, u32[]{:S(2)}) collective-permute-start(bf16[192,896]{1,0:T(8,128)(2,1)S(1)} %collective-permute-done.2), channel_id=1, source_target_pairs={{0,64},{64,128},{128,192},{192,256},{256,320},{320,384},{384,448},... | collective-permute-start | bytes 1032200 | tf_op jit(solution)/shard_map/ppermute | solution.py:48
  75.9 10.3 %collective-permute-start.4 = (bf16[192,896]{1,0:T(8,128)(2,1)S(1)}, bf16[192,896]{1,0:T(8,128)(2,1)S(1)}, u32[]{:S(2)}, u32[]{:S(2)}) collective-permute-start(bf16[192,896]{1,0:T(8,128)(2,1)S(1)} %collective-permute-done.3), channel_id=1, source_target_pairs={{0,64},{64,128},{128,192},{192,256},{256,320},{320,384},{384,448},... | collective-permute-start | bytes 1032200 | tf_op jit(solution)/shard_map/ppermute | solution.py:48
  86.2 10.3 %collective-permute-start.5 = (bf16[192,896]{1,0:T(8,128)(2,1)S(1)}, bf16[192,896]{1,0:T(8,128)(2,1)S(1)}, u32[]{:S(2)}, u32[]{:S(2)}) collective-permute-start(bf16[192,896]{1,0:T(8,128)(2,1)S(1)} %collective-permute-done.4), channel_id=1, source_target_pairs={{0,64},{64,128},{128,192},{192,256},{256,320},{320,384},{384,448},... | collective-permute-start | bytes 1032200 | tf_op jit(solution)/shard_map/ppermute | solution.py:48
  88.2 170.7 %reduce-scatter.2.cloned.1.call-start = ((), (), s32[]{:S(2)}) async-start(), calls=%async_computation.3 | async-start | bytes 3342336 | tf_op jit(solution)/shard_map/reduce_scatter | solution.py:65
  96.6 10.3 %collective-permute-start.6 = (bf16[192,896]{1,0:T(8,128)(2,1)S(1)}, bf16[192,896]{1,0:T(8,128)(2,1)S(1)}, u32[]{:S(2)}, u32[]{:S(2)}) collective-permute-start(bf16[192,896]{1,0:T(8,128)(2,1)S(1)} %collective-permute-done.5), channel_id=1, source_target_pairs={{0,64},{64,128},{128,192},{192,256},{256,320},{320,384},{384,448},... | collective-permute-start | bytes 1032200 | tf_op jit(solution)/shard_map/ppermute | solution.py:48
  119.5 4.3 %copy-start = (bf16[1,512,896]{1,2,0:T(8,128)(2,1)S(1)}, bf16[1,512,896]{1,2,0:T(8,128)(2,1)}, u32[]{:S(2)}) copy-start(bf16[1,512,896]{1,2,0:T(8,128)(2,1)} %copy.18) | copy-start | bytes 2752516
  154.2 104.6 %copy-start.1 = (bf16[1,96,512]{2,1,0:T(8,128)(2,1)S(1)}, bf16[1,96,512]{2,1,0:T(8,128)(2,1)}, u32[]{:S(2)}) copy-start(bf16[1,96,512]{2,1,0:T(8,128)(2,1)} %param.10) | copy-start | bytes 294916
  154.3 111.0 %copy-start.2 = (bf16[1,1536,512]{2,1,0:T(8,128)(2,1)S(1)}, bf16[1,1536,512]{2,1,0:T(8,128)(2,1)}, u32[]{:S(2)}) copy-start(bf16[1,1536,512]{2,1,0:T(8,128)(2,1)} %all-gather.3.cloned.1.call-done) | copy-start | bytes 4718596
  259.8 10.2 %collective-permute-start.7 = (bf16[96,512]{1,0:T(8,128)(2,1)S(1)}, bf16[96,512]{1,0:T(8,128)(2,1)S(1)}, u32[]{:S(2)}, u32[]{:S(2)}) collective-permute-start(bf16[96,512]{1,0:T(8,128)(2,1)S(1)} %fusion.36), channel_id=1, source_target_pairs={{16,0},{32,16},{48,32},{17,1},{33,17},{49,33},{18,2},{34,18},{50,3... | collective-permute-start | bytes 294920 | tf_op jit(solution)/shard_map/ppermute | solution.py:10
Sparse Core Ops, SparseCore 0:
  10.1 64.5 all-gather.4
  88.3 65.5 all-gather.2
  158.8 99.9 reduce-scatter.1
